TPU v7x, 256 devices: a whole 4x4x8 slice. The times are simulated.
256 devices in a mesh: tm: 16 (over x_lo, z), sensor: 16 (over x_hi, y, core).
Axes of the slice: x: 4 (x_hi: 2, x_lo: 2; x = x_hi * 2 + x_lo), y: 4, z: 8, core: 2. Of those that a mesh axis runs over, the one named last changes fastest.
Arguments:
- state_tiles: bfloat16 [32768, 8192], P('sensor', 'tm'), may hold values from -6 to 6
- sketch: bfloat16 [1024, 128], replicated, may hold values from -0.1875 to 0.1875
- probe_cell: int32 [16, 16, 32], P('sensor'), may hold values from 0 to 2047
- probe_row: int32 [16, 16, 32], P('sensor'), may hold values from -1 to 255, as said below
Outputs:
- hankel_sketch: float32 [512, 4096, 128], P('tm', 'sensor')
- column_image: float32 [1024, 128], P(('tm', 'sensor'))
Inputs may be any that keep to these rules, and one draw needn't show every extreme that they name: `probe_row`: every sensor row of every owner is filled by exactly one slot over all tiles; for each owner, the tiles that feed it fill all 32 of their slots to it and the other tiles none, and exactly half of the tiles feed each owner.
All inputs are finite; a program needn't handle non-finite values.
Results may differ from a plain program's by a relative error of at most 0.0003.
Values may be sent and summed in bfloat16 or wider, within the bound.
A program may use at most 64 MiB of HBM per device.

v0:
```python
import math

import jax
import jax.numpy as jnp
from jax import lax
from jax.sharding import PartitionSpec as P

INPUTS = 16
SENS_DEV = 256


def shifted(x, axis, by):
    count = lax.axis_size(axis)
    pairs = [(i, i + by) for i in range(count) if 0 <= i + by < count]
    return lax.ppermute(x, axis, pairs)


def local(state_tiles, sketch, probe_cell, probe_row):
    n_tiles = lax.axis_size("sensor")
    cells_here = state_tiles.shape[0]
    width = state_tiles.shape[1]
    steps_here = width // INPUTS
    capacity = probe_cell.shape[2]
    cell_index = probe_cell[0].reshape(-1)
    onehot = (cell_index[:, None] == jnp.arange(cells_here, dtype=jnp.int32)[None, :]).astype(
        jnp.bfloat16
    )
    picked = jnp.dot(onehot, state_tiles, preferred_element_type=jnp.float32).astype(jnp.bfloat16)
    picked = picked.reshape(n_tiles, capacity, width)
    arrived = lax.all_to_all(picked, "sensor", split_axis=0, concat_axis=0, tiled=True)
    row_index = probe_row[0].reshape(-1)
    placement = (row_index[None, :] == jnp.arange(SENS_DEV, dtype=jnp.int32)[:, None]).astype(
        jnp.bfloat16
    )
    own_block = jnp.dot(
        placement, arrived.reshape(n_tiles * capacity, width), preferred_element_type=jnp.float32
    ).astype(jnp.bfloat16)
    next_one = shifted(own_block, "tm", -1)
    next_two = shifted(own_block, "tm", -2)
    extended = jnp.concatenate([own_block, next_one, next_two], axis=1)
    span = sketch.shape[0]
    group_size = math.gcd(steps_here, 8)
    total = jnp.zeros((span, sketch.shape[1]), jnp.float32)
    pieces = []
    for block in range(steps_here // group_size):
        windows = jnp.stack(
            [
                extended[
                    :,
                    (block * group_size + offset) * INPUTS : (block * group_size + offset) * INPUTS
                    + span,
                ]
                for offset in range(group_size)
            ]
        )
        image = jnp.einsum("isk,kc->isc", windows, sketch, preferred_element_type=jnp.float32)
        image_bf = image.astype(jnp.bfloat16)
        total = total + jnp.einsum(
            "isk,isc->kc", windows, image_bf, preferred_element_type=jnp.float32
        )
        pieces.append(image)
    hankel_sketch = jnp.concatenate(pieces, axis=0)
    norm_scale = 1.0 / math.sqrt(SENS_DEV * n_tiles * steps_here * lax.axis_size("tm"))
    total = total * norm_scale
    column_image = lax.psum_scatter(total, ("tm", "sensor"), scatter_dimension=0, tiled=True)
    return (hankel_sketch, column_image)


def solution(mesh):
    placed = (P("sensor", "tm"), P(), P("sensor", None, None), P("sensor", None, None))
    return jax.shard_map(
        local,
        mesh=mesh,
        in_specs=placed,
        out_specs=(P("tm", "sensor", None), P(("tm", "sensor"), None)),
        check_vma=False,
    )
```

profile of v0, /device:TPU:1, one launch (start us, length us, event | category | flops | bytes accessed | tf_op | source)
XLA Modules:
  0.0 333.8 jit_solution(5028198542764452020)
XLA Ops:
  7.2 0.0 copy-start
  7.2 0.9 eq.34
  8.1 0.7 copy-done
  8.8 0.0 copy-start.5
  8.8 2.1 fusion.2
  10.9 8.4 %all-to-all-start = ((bf16[16,32,512]{2,1,0:T(8,128)(2,1)}), bf16[16,32,512]{2,1,0:T(8,128)(2,1)S(1)}, u32[]{:S(2)}, u32[]{:S(2)}) async-start(bf16[16,32,512]{2,1,0:T(8,128)(2,1)} %bitcast), calls=%async_computation | async-start | bytes 1048576 | tf_op jit(solution)/shard_map/all_to_all | solution.py:30
  19.3 0.0 all-reduce.3.cloned.1.call-start
  19.3 0.0 copy-done.5
  19.4 0.1 eq.30
  19.4 11.0 %all-to-all-done = bf16[16,32,512]{2,1,0:T(8,128)(2,1)S(1)} async-done(((bf16[16,32,512]{2,1,0:T(8,128)(2,1)}), bf16[16,32,512]{2,1,0:T(8,128)(2,1)S(1)}, u32[]{:S(2)}, u32[]{:S(2)}) %all-to-all-start) | async-done | bytes 524320 | tf_op jit(solution)/shard_map/all_to_all | solution.py:30
  30.5 0.3 convolution_convert_fusion
  30.8 1.3 collective-permute-start
  32.1 1.3 collective-permute-start.1
  33.4 6.3 %collective-permute-done = bf16[256,512]{1,0:T(8,128)(2,1)S(1)} collective-permute-done((bf16[256,512]{1,0:T(8,128)(2,1)S(1)}, bf16[256,512]{1,0:T(8,128)(2,1)S(1)}, u32[]{:S(2)}, u32[]{:S(2)}) %collective-permute-start) | collective-permute-done | bytes 262176 | tf_op jit(solution)/shard_map/ppermute | solution.py:15
  39.6 12.6 %collective-permute-done.1 = bf16[256,512]{1,0:T(8,128)(2,1)S(1)} collective-permute-done((bf16[256,512]{1,0:T(8,128)(2,1)S(1)}, bf16[256,512]{1,0:T(8,128)(2,1)S(1)}, u32[]{:S(2)}, u32[]{:S(2)}) %collective-permute-start.1) | collective-permute-done | bytes 262176 | tf_op jit(solution)/shard_map/ppermute | solution.py:15
  52.2 0.1 pad_maximum_fusion.1
  52.3 0.2 fusion.30
  52.5 0.1 fusion.38
  52.5 1.0 fusion.37
  53.5 1.0 fusion.36
  54.5 1.0 fusion.35
  55.4 1.0 fusion.34
  56.4 1.0 fusion.33
  57.4 0.0 copy-start.4
  57.4 1.0 fusion.32
  58.4 1.0 fusion.31
  59.4 0.0 copy-done.4
  59.4 1.3 fusion.47
  60.6 0.0 copy-start.1
  60.6 1.3 convolution_bitcast_fusion.2
  62.0 1.3 fusion.45
  63.2 0.0 copy-done.1
  63.2 0.0 copy-start.2
  63.2 1.3 convolution_bitcast_fusion.1
  64.6 1.5 fusion.43
  66.0 0.0 copy-done.2
  66.0 0.0 copy-start.3
  66.0 1.3 convolution_bitcast_fusion
  67.3 0.0 copy-done.3
  67.3 1.3 fusion.49
  68.6 2.2 fusion.6
  70.8 0.0 all-reduce.3.cloned.1.call-update
  70.8 4.3 %pad_maximum_fusion = f32[32,256,128]{2,1,0:T(8,128)} fusion(f32[8,256,128]{2,1,0:T(8,128)} %copy-done.3, f32[8,256,128]{2,1,0:T(8,128)} %copy-done.2, f32[8,256,128]{2,1,0:T(8,128)} %copy-done.1, f32[8,256,128]{2,1,0:T(8,128)S(1)} %fusion.49), kind=kLoop, calls=%fused_computation | loop fusion | flops 3145728 | bytes 8388608 | tf_op jit(solution)/shard_map/concatenate | solution.py:62
  75.1 250.6 %all-reduce.3.cloned.1.call-done = f32[1024,128]{1,0:T(8,128)} async-done(((f32[1024,128]{1,0:T(8,128)}), f32[1024,128]{1,0:T(8,128)}) %all-reduce.3.cloned.1.call-update) | async-done | bytes 524304
  325.7 1.3 constant_dynamic-slice_fusion
Async XLA Ops:
  7.2 1.6 copy-start
  8.8 10.6 %copy-start.5 = (s32[1,16,32]{2,1,0:T(8,128)S(1)}, s32[1,16,32]{2,1,0:T(8,128)}, u32[]{:S(2)}) copy-start(s32[1,16,32]{2,1,0:T(8,128)} %param.7) | copy-start | bytes 6148
  10.9 19.6 %all-to-all-start = ((bf16[16,32,512]{2,1,0:T(8,128)(2,1)}), bf16[16,32,512]{2,1,0:T(8,128)(2,1)S(1)}, u32[]{:S(2)}, u32[]{:S(2)}) async-start(bf16[16,32,512]{2,1,0:T(8,128)(2,1)} %bitcast), calls=%async_computation | async-start | bytes 1048576 | tf_op jit(solution)/shard_map/all_to_all | solution.py:30
  19.3 306.4 %all-reduce.3.cloned.1.call-start = ((), (), s32[]{:S(2)}) async-start(), calls=%async_computation.1 | async-start | bytes 1048576
  30.8 8.9 %collective-permute-start = (bf16[256,512]{1,0:T(8,128)(2,1)S(1)}, bf16[256,512]{1,0:T(8,128)(2,1)S(1)}, u32[]{:S(2)}, u32[]{:S(2)}) collective-permute-start(bf16[256,512]{1,0:T(8,128)(2,1)S(1)} %convolution_convert_fusion), channel_id=1, source_target_pairs={{16,0},{32,16},{48,32},{64,48},{80,64},{96,80},{112,96},{128,112},... | collective-permute-start | bytes 786440 | tf_op jit(solution)/shard_map/ppermute | solution.py:15
  32.1 20.1 %collective-permute-start.1 = (bf16[256,512]{1,0:T(8,128)(2,1)S(1)}, bf16[256,512]{1,0:T(8,128)(2,1)S(1)}, u32[]{:S(2)}, u32[]{:S(2)}) collective-permute-start(bf16[256,512]{1,0:T(8,128)(2,1)S(1)} %convolution_convert_fusion), channel_id=1, source_target_pairs={{32,0},{48,16},{64,32},{80,48},{96,64},{112,80},{128,96},{144,112}... | collective-permute-start | bytes 786440 | tf_op jit(solution)/shard_map/ppermute | solution.py:15
  57.4 2.0 copy-start.4
  60.6 2.6 copy-start.1
  63.2 2.8 copy-start.2
  66.0 1.3 copy-start.3
Sparse Core Ops, SparseCore 0:
  70.9 254.7 all-reduce.2
where the time goes:
time: 335 us; the launch traced here: 334 us
  waiting for transfers between devices  280 us (84%)
  between operations  14.3 us (4%)
  matrix products  13.7 us (4%)
  starting transfers between devices  11.1 us (3%)
  local copies, waits for them, and re-layouts  9.89 us (3%)
  other arithmetic  4.43 us (1%)
    unnamed x2, waiting for transfers between devices  251 us
    ppermute x2, waiting for transfers between devices, shifted(): return lax.ppermute(x, axis, pairs)  18.8 us
    all_to_all x1, waiting for transfers between devices, local(): lax.all_to_all(picked, 'sensor', split_axis=0, concat_axis=0, tiled=True)  11 us
    all_to_all x1, starting transfers between devices, local(): lax.all_to_all(picked, 'sensor', split_axis=0, concat_axis=0, tiled=True)  8.43 us
    unnamed x20, local copies, waits for them, and re-layouts  7.93 us
  transfers between devices with their start and end apart: 4, of which 4 were waited for; matrix products, arithmetic and copies ran while one was open for 1% of the time, Pallas kernels for 0%

commit v1 on v0

v1 whole, which is shorter than its diff:
```python
import functools
import math

import jax
import jax.numpy as jnp
from jax import lax
from jax.experimental import pallas as pl
from jax.experimental.pallas import tpu as pltpu
from jax.sharding import PartitionSpec as P

INPUTS = 16
KC = 64
LANES = 128
MESH = pl.DeviceIdType.MESH
F32 = jnp.float32
BF16 = jnp.bfloat16


def dot(a, b):
    return jnp.dot(a, b, preferred_element_type=F32)


def kernel(
    n_tm, n_sn, n_xl, n_xh, scale,
    state, sketch, cell, row, hank, col,
    st, sk, cellv, rowv, one, put, sendb, arr, hx, ht, big, hb, rb, acc2, tot, s0b, mid, s1b, m2, s2b,
    ld_sem, a_send, a_recv, h_send, h_recv, out_sem, s0_send, s0_recv, s1_send, s1_recv, s2_send, s2_recv,
):
    t = lax.axis_index("tm")
    s = lax.axis_index("sensor")
    n_z = n_tm // n_xl
    n_xy = n_sn // 2
    zh = n_z // 2
    xl = t // n_z
    z = lax.rem(t, n_z)
    xy = s // 2
    k = lax.rem(s, 2)
    cap = cellv.shape[2]
    sd = hx.shape[1]
    span = sk.shape[0]
    cells = st.shape[0]

    loads = [
        pltpu.make_async_copy(cell, cellv, ld_sem.at[0]),
        pltpu.make_async_copy(row, rowv, ld_sem.at[1]),
        pltpu.make_async_copy(state.at[:, pl.ds(0, 256)], st.at[:, pl.ds(0, 256)], ld_sem.at[2]),
        pltpu.make_async_copy(state.at[:, pl.ds(256, 256)], st.at[:, pl.ds(256, 256)], ld_sem.at[3]),
        pltpu.make_async_copy(sketch, sk, ld_sem.at[4]),
    ]
    for c in loads:
        c.start()

    barrier = pltpu.get_barrier_semaphore()

    def greet(tt, ss):
        pl.semaphore_signal(barrier, inc=1, device_id=(tt, ss), device_id_type=MESH)

    def greet_sensor(d, _):
        greet(t, lax.rem(s + d, n_sn))
        return 0

    lax.fori_loop(1, n_sn, greet_sensor, 0)

    @pl.when(t > 0)
    def _():
        greet(t - 1, s)

    @pl.when(t < n_tm - 1)
    def _():
        greet(t + 1, s)

    def greet_plane(d, _):
        e = lax.rem(xl * n_xy + xy + d, n_xl * n_xy)
        greet((e // n_xy) * n_z + z, lax.rem(e, n_xy) * 2 + k)
        return 0

    lax.fori_loop(1, n_xl * n_xy, greet_plane, 0)

    def greet_line(d, _):
        e = lax.rem(z * 2 + k + d, n_z * 2)
        greet(xl * n_z + e // 2, xy * 2 + lax.rem(e, 2))
        return 0

    lax.fori_loop(1, n_z * 2, greet_line, 0)
    n_greet = n_sn - 1 + n_xl * n_xy - 1 + n_z * 2 - 1

    loads[0].wait()
    eye = lax.broadcasted_iota(jnp.int32, (cap, cap), 0) == lax.broadcasted_iota(jnp.int32, (cap, cap), 1)

    def column(ref, o):
        line = ref[0, o : o + 1, :].astype(F32)
        return jnp.sum(jnp.where(eye, jnp.broadcast_to(line, (cap, cap)), 0.0), axis=1, keepdims=True)

    lane_cells = lax.broadcasted_iota(jnp.int32, (cap, cells), 1).astype(F32)
    for o in range(n_sn):
        one[o * cap : (o + 1) * cap, :] = jnp.where(column(cellv, o) == lane_cells, 1.0, 0.0).astype(BF16)

    def pick(half):
        res = dot(one[...], st[:, 256 * half : 256 * half + 256]).astype(BF16)
        sendb[2 * half] = res[:, :LANES]
        sendb[2 * half + 1] = res[:, LANES:]

    def a_copy(q, d):
        dst = lax.rem(s + d, n_sn)
        return pltpu.make_async_remote_copy(
            src_ref=sendb.at[q, pl.ds(pl.multiple_of(dst * cap, cap), cap)],
            dst_ref=arr.at[q, pl.ds(pl.multiple_of(s * cap, cap), cap)],
            send_sem=a_send.at[q, d],
            recv_sem=a_recv.at[q, s],
            device_id=(t, dst),
            device_id_type=MESH,
        )

    def a_arrival(q, src):
        return pltpu.make_async_remote_copy(
            src_ref=sendb.at[q, pl.ds(pl.multiple_of(src * cap, cap), cap)],
            dst_ref=arr.at[q, pl.ds(pl.multiple_of(src * cap, cap), cap)],
            send_sem=a_send.at[q, 0],
            recv_sem=a_recv.at[q, src],
            device_id=(t, src),
            device_id_type=MESH,
        )

    def exchange(q):
        def body(d, _):
            a_copy(q, d).start()
            return 0

        lax.fori_loop(1, n_sn, body, 0)
        own = pl.ds(pl.multiple_of(s * cap, cap), cap)
        arr[q, own] = sendb[q, own]

    loads[2].wait()
    pick(0)
    pl.semaphore_wait(barrier, n_greet + jnp.where(t > 0, 1, 0) + jnp.where(t < n_tm - 1, 1, 0))
    exchange(0)
    exchange(1)
    loads[3].wait()
    pick(1)
    exchange(2)
    exchange(3)

    loads[1].wait()
    lane_rows = lax.broadcasted_iota(jnp.int32, (cap, sd), 1).astype(F32)
    for o in range(n_sn):
        hit = jnp.where(column(rowv, o) == lane_rows, 1.0, 0.0).astype(BF16)
        one[o * cap : (o + 1) * cap, :sd] = hit
    put[...] = jnp.transpose(one[: n_sn * cap, :sd])

    loads[4].wait()
    for i in range(8):
        cols = pl.ds(LANES * i, LANES)
        if i > 0:
            big[: INPUTS * i, cols] = jnp.zeros((INPUTS * i, LANES), BF16)
        big[INPUTS * i : INPUTS * i + span, cols] = sk[...]
        big[INPUTS * i + span :, cols] = jnp.zeros((LANES - INPUTS * i, LANES), BF16)

    @pl.when(t >= n_tm - 2)
    def _():
        hx[8:12] = jnp.zeros((4, sd, LANES), BF16)
        ht[8 * LANES :, :] = jnp.zeros((4 * LANES, sd), BF16)

    @pl.when(t == n_tm - 1)
    def _():
        hx[4:8] = jnp.zeros((4, sd, LANES), BF16)
        ht[4 * LANES : 8 * LANES, :] = jnp.zeros((4 * LANES, sd), BF16)

    def h_copy(c):
        return pltpu.make_async_remote_copy(
            src_ref=hx.at[c],
            dst_ref=hx.at[c + 4],
            send_sem=h_send.at[c],
            recv_sem=h_recv.at[c],
            device_id=(jnp.maximum(t - 1, 0), s),
            device_id_type=MESH,
        )

    def turn(c):
        ht[LANES * c : LANES * (c + 1), :] = jnp.transpose(hx[c])

    def place(q):
        def body(d, _):
            a_arrival(q, lax.rem(s + d, n_sn)).wait_recv()
            return 0

        lax.fori_loop(1, n_sn, body, 0)
        hx[q] = dot(put[...], arr[q]).astype(BF16)

        @pl.when(t > 0)
        def _():
            h_copy(q).start()

        turn(q)

    def relay(q):
        @pl.when(t < n_tm - 1)
        def _():
            h_copy(q).wait_recv()

            @pl.when(t > 0)
            def _():
                h_copy(4 + q).start()

            turn(4 + q)

    def part(u, chunks, first):
        lhs = jnp.concatenate([hx[c] for c in chunks], axis=1)
        low = LANES * (chunks[0] - u)
        for v in range(4):
            r = dot(lhs, big[low : low + LANES * len(chunks), 256 * v : 256 * v + 256])
            for i in range(2):
                piece = r[:, LANES * i : LANES * (i + 1)]
                hb[u, 2 * v + i] = piece if first else hb[u, 2 * v + i] + piece

    place(0)
    place(1)
    relay(0)
    place(2)
    relay(1)
    place(3)
    for u in range(4):
        part(u, list(range(u, 4)), True)
    relay(2)
    relay(3)
    for u in range(4):
        part(u, [4, 5, 6, 7], False)

    def out_copy(u):
        return pltpu.make_async_copy(hb.at[u], hank.at[pl.ds(8 * u, 8)], out_sem.at[u])

    for u in range(4):
        @pl.when(t < n_tm - 2)
        def _():
            h_copy(4 + u).wait_recv()
            turn(8 + u)

        chunks = list(range(8, 9 + u))
        lhs = jnp.concatenate([hx[c] for c in chunks], axis=1)
        low = LANES * (8 - u)
        for v in range(4):
            r = dot(lhs, big[low : low + LANES * len(chunks), 256 * v : 256 * v + 256])
            r = r + jnp.concatenate([hb[u, 2 * v], hb[u, 2 * v + 1]], axis=1)
            hb[u, 2 * v] = r[:, :LANES]
            hb[u, 2 * v + 1] = r[:, LANES:]
            rb[v * sd : (v + 1) * sd, :] = r.astype(BF16)
        out_copy(u).start()
        rows = span + INPUTS
        lhs = jnp.concatenate([ht[LANES * u + 32 * v : LANES * u + 32 * v + rows, :] for v in range(4)], axis=1)
        grown = dot(lhs, rb[...])
        acc2[...] = grown if u == 0 else acc2[...] + grown

    tr = tot.shape[3]
    whole = acc2[:span, :LANES] + acc2[INPUTS : INPUTS + span, LANES:]
    tot[...] = whole.reshape(tot.shape)

    def s0_copy(a):
        return pltpu.make_async_remote_copy(
            src_ref=tot.at[a, pl.ds((1 - k) * zh, zh)],
            dst_ref=s0b.at[a],
            send_sem=s0_send.at[a],
            recv_sem=s0_recv.at[a],
            device_id=(t, s + 1 - 2 * k),
            device_id_type=MESH,
        )

    for a in range(n_xl):
        s0_copy(a).start()

    me = xl * n_xy + xy

    def s1_copy(a, b):
        return pltpu.make_async_remote_copy(
            src_ref=mid.at[a, b],
            dst_ref=s1b.at[me],
            send_sem=s1_send.at[a, b],
            recv_sem=s1_recv.at[me],
            device_id=(a * n_z + z, b * 2 + k),
            device_id_type=MESH,
        )

    def s1_arrival(e):
        return pltpu.make_async_remote_copy(
            src_ref=mid.at[0, 0],
            dst_ref=s1b.at[e],
            send_sem=s1_send.at[0, 0],
            recv_sem=s1_recv.at[e],
            device_id=(t, s),
            device_id_type=MESH,
        )

    for a in range(n_xl):
        s0_copy(a).wait_recv()
        for c in range(zh):
            mid[a, :, c] = tot[a, k * zh + c] + s0b[a, c]

        def body(d, _):
            b = lax.rem(xy + d, n_xy)

            @pl.when((a != xl) | (b != xy))
            def _():
                s1_copy(a, b).start()

            return 0

        lax.fori_loop(0, n_xy, body, 0)

    s1b[me] = mid[xl, xy]

    def s1_wait(d, _):
        s1_arrival(lax.rem(me + d, n_xl * n_xy)).wait_recv()
        return 0

    lax.fori_loop(1, n_xl * n_xy, s1_wait, 0)
    m2[...] = jnp.sum(s1b[...], axis=0)

    def s2_copy(c, kk):
        return pltpu.make_async_remote_copy(
            src_ref=m2.at[c],
            dst_ref=s2b.at[z],
            send_sem=s2_send.at[c, kk],
            recv_sem=s2_recv.at[z],
            device_id=(xl * n_z + k * zh + c, s - k + kk),
            device_id_type=MESH,
        )

    def s2_arrival(e):
        return pltpu.make_async_remote_copy(
            src_ref=m2.at[0],
            dst_ref=s2b.at[e],
            send_sem=s2_send.at[0, 0],
            recv_sem=s2_recv.at[e],
            device_id=(t, s),
            device_id_type=MESH,
        )

    for c in range(zh):
        for kk in range(2):
            @pl.when((k * zh + c != z) | (k != kk))
            def _():
                s2_copy(c, kk).start()

    @pl.when(z // zh == k)
    def _():
        s2b[z] = m2[z - k * zh]

    for e in range(n_z):
        @pl.when((e != z) | (z // zh != k))
        def _():
            s2_arrival(e).wait_recv()

    done = jnp.sum(s2b[...], axis=0)
    half = tr // 2
    col[...] = jnp.where(k == 0, done[:half], done[half:]) * scale

    for u in range(4):
        out_copy(u).wait()
    for q in range(4):
        def body(d, _):
            a_copy(q, d).wait_send()
            return 0

        lax.fori_loop(1, n_sn, body, 0)

    @pl.when(t > 0)
    def _():
        for q in range(4):
            h_copy(q).wait_send()

    @pl.when((t > 0) & (t < n_tm - 1))
    def _():
        for q in range(4):
            h_copy(4 + q).wait_send()

    for a in range(n_xl):
        s0_copy(a).wait_send()

        def body(b, _):
            @pl.when((a != xl) | (b != xy))
            def _():
                s1_copy(a, b).wait_send()

            return 0

        lax.fori_loop(0, n_xy, body, 0)
    for c in range(zh):
        for kk in range(2):
            @pl.when((k * zh + c != z) | (k != kk))
            def _():
                s2_copy(c, kk).wait_send()


def solution(mesh):
    n_tm, n_sn = mesh.shape["tm"], mesh.shape["sensor"]
    n_xl = 2
    n_z = n_tm // n_xl
    n_xy = n_sn // 2

    def local(state, sketch, cell, row):
        cells, width = state.shape
        span, cols = sketch.shape
        cap = cell.shape[2]
        sd = n_sn * cap // 2
        steps = width // INPUTS
        slots = n_sn * cap
        own_rows = span // (n_tm * n_sn)
        tr = 2 * own_rows
        zh = n_z // 2
        scale = 1.0 / math.sqrt(sd * n_sn * steps * n_tm)
        hbm = pl.BlockSpec(memory_space=pltpu.HBM)
        dma = pltpu.SemaphoreType.DMA
        return pl.pallas_call(
            functools.partial(kernel, n_tm, n_sn, n_xl, 1, scale),
            out_shape=(
                jax.ShapeDtypeStruct((steps, sd, cols), F32),
                jax.ShapeDtypeStruct((own_rows, cols), F32),
            ),
            in_specs=[hbm] * 4,
            out_specs=(hbm, pl.BlockSpec(memory_space=pltpu.VMEM)),
            scratch_shapes=[
                pltpu.VMEM((cells, width), BF16),
                pltpu.VMEM((span, cols), BF16),
                pltpu.VMEM(cell.shape, jnp.int32),
                pltpu.VMEM(row.shape, jnp.int32),
                pltpu.VMEM((slots, cells), BF16),
                pltpu.VMEM((sd, slots), BF16),
                pltpu.VMEM((4, slots, LANES), BF16),
                pltpu.VMEM((4, slots, LANES), BF16),
                pltpu.VMEM((12, sd, LANES), BF16),
                pltpu.VMEM((12 * LANES, sd), BF16),
                pltpu.VMEM((span + LANES, 8 * LANES), BF16),
                pltpu.VMEM((4, 8, sd, LANES), F32),
                pltpu.VMEM((4 * sd, 2 * LANES), BF16),
                pltpu.VMEM((span + INPUTS, 2 * LANES), F32),
                pltpu.VMEM((n_xl, n_z, n_xy, tr, LANES), F32),
                pltpu.VMEM((n_xl, zh, n_xy, tr, LANES), F32),
                pltpu.VMEM((n_xl, n_xy, zh, tr, LANES), F32),
                pltpu.VMEM((n_xl * n_xy, zh, tr, LANES), F32),
                pltpu.VMEM((zh, tr, LANES), F32),
                pltpu.VMEM((n_z, tr, LANES), F32),
                dma((5,)),
                dma((4, n_sn)),
                dma((4, n_sn)),
                dma((8,)),
                dma((8,)),
                dma((4,)),
                dma((n_xl,)),
                dma((n_xl,)),
                dma((n_xl, n_xy)),
                dma((n_xl * n_xy,)),
                dma((zh, 2)),
                dma((n_z,)),
            ],
            compiler_params=pltpu.CompilerParams(
                collective_id=0, has_side_effects=True, vmem_limit_bytes=63 * 2**20
            ),
        )(state, sketch, cell, row)

    placed = (P("sensor", "tm"), P(), P("sensor", None, None), P("sensor", None, None))
    return jax.shard_map(
        local,
        mesh=mesh,
        in_specs=placed,
        out_specs=(P("tm", "sensor", None), P(("tm", "sensor"), None)),
        check_vma=False,
    )
```

time: 335 us -> 54.8 us (0.16)
  waiting for transfers between devices: 280 us -> 0 us
  Pallas kernels: 0 us -> 48.9 us
  matrix products: 13.7 us -> 0 us
  between operations: 14.3 us -> 0.65 us
  starting transfers between devices: 11.1 us -> 0 us
  local copies, waits for them, and re-layouts: 9.89 us -> 5.24 us
  other arithmetic: 4.43 us -> 0 us
    unnamed x2 -> x0, waiting for transfers between devices: 251 us -> none
    pallas_call x0 -> x1, Pallas kernels: none -> 48.9 us  [local(): pl.pallas_call(functools.partial(kernel, n_tm, n_sn, n_xl, 1, scale), out...]
    ppermute x2 -> x0, waiting for transfers between devices: 18.8 us -> none  [shifted(): return lax.ppermute(x, axis, pairs)]
    dot_general x10 -> x0, matrix products: 13.7 us -> none  [the longest x4 6.07 us: local(): jnp.einsum('isk,isc->kc', windows, image_bf, preferred_element_type=jnp.f...]
    all_to_all x1 -> x0, waiting for transfers between devices: 11 us -> none  [local(): lax.all_to_all(picked, 'sensor', split_axis=0, concat_axis=0, tiled=True)]
    all_to_all x1 -> x0, starting transfers between devices: 8.43 us -> none  [local(): lax.all_to_all(picked, 'sensor', split_axis=0, concat_axis=0, tiled=True)]
    concatenate x2 -> x0, other arithmetic: 4.38 us -> none  [the longest x1 4.33 us: local(): hankel_sketch = jnp.concatenate(pieces, axis=0)]
    unnamed x20 -> x4, local copies, waits for them, and re-layouts: 7.93 us -> 5.24 us
  transfers between devices with their start and end apart: 4 -> 0, of which waited for: 4 -> 0; matrix products, arithmetic and copies ran while one was open for 1% -> 0% of each run, Pallas kernels for 0% -> 0%
where the time goes in v1:
time: 54.8 us; the launch traced here: 54.7 us
  Pallas kernels  48.9 us (89%)
  local copies, waits for them, and re-layouts  5.24 us (10%)
  between operations  0.65 us (1%)
    pallas_call x1, Pallas kernels, local(): pl.pallas_call(functools.partial(kernel, n_tm, n_sn, n_xl, 1, scale), out...  48.9 us
    unnamed x4, local copies, waits for them, and re-layouts  5.24 us

profile of v1, /device:TPU:1, one launch (start us, length us, event | category | flops | bytes accessed | tf_op | source)
XLA Modules:
  0.0 54.7 jit_solution(942574913308582867)
XLA Ops:
  0.6 48.9 %shard_map.59 = (f32[32,256,128]{2,1,0:T(8,128)}, f32[4,128]{1,0:T(4,128)}) custom-call(bf16[2048,512]{1,0:T(8,128)(2,1)} %state.1, bf16[1024,128]{1,0:T(8,128)(2,1)} %sketch.1, s32[1,16,32]{2,1,0:T(8,128)} %cell.1, s32[1,16,32]{2,1,0:T(8,128)} %row.1), custom_call_target="tpu_custom_call" | custom-call | tf_op jit(solution)/shard_map/pallas_call | solution.py:411
  49.5 0.0 copy-start
  49.5 4.7 %copy.8 = f32[32,256,128]{2,1,0:T(8,128)} copy(f32[32,256,128]{2,1,0:T(8,128)} %get-tuple-element.4) | data formatting | bytes 8388608
  54.2 0.0 copy-done
  54.2 0.6 %copy.9 = f32[4,128]{1,0:T(4,128)} copy(f32[4,128]{1,0:T(4,128)S(1)} %copy-done) | data formatting | bytes 4096
Async XLA Ops:
  49.5 4.7 %copy-start = (f32[4,128]{1,0:T(4,128)S(1)}, f32[4,128]{1,0:T(4,128)}, u32[]{:S(2)}) copy-start(f32[4,128]{1,0:T(4,128)} %get-tuple-element.5) | copy-start | bytes 6148

commit v2 on v1

--- a/solution.py
+++ b/solution.py
@@ -55,34 +55,27 @@
     def greet(tt, ss):
         pl.semaphore_signal(barrier, inc=1, device_id=(tt, ss), device_id_type=MESH)
 
+    def greet_line(d, _):
+        greet(xl * n_z + lax.rem(z + d, n_z), 2 * xy + z // zh)
+        return 0
+
     def greet_sensor(d, _):
         greet(t, lax.rem(s + d, n_sn))
         return 0
 
+    def greet_plane(b, _):
+        greet(lax.rem(t + n_z, n_tm), 2 * b + k)
+        return 0
+
     lax.fori_loop(1, n_sn, greet_sensor, 0)
-
-    @pl.when(t > 0)
-    def _():
-        greet(t - 1, s)
+    lax.fori_loop(1, n_z, greet_line, 0)
+    lax.fori_loop(0, n_xy, greet_plane, 0)
 
     @pl.when(t < n_tm - 1)
     def _():
         greet(t + 1, s)
 
-    def greet_plane(d, _):
-        e = lax.rem(xl * n_xy + xy + d, n_xl * n_xy)
-        greet((e // n_xy) * n_z + z, lax.rem(e, n_xy) * 2 + k)
-        return 0
-
-    lax.fori_loop(1, n_xl * n_xy, greet_plane, 0)
-
-    def greet_line(d, _):
-        e = lax.rem(z * 2 + k + d, n_z * 2)
-        greet(xl * n_z + e // 2, xy * 2 + lax.rem(e, 2))
-        return 0
-
-    lax.fori_loop(1, n_z * 2, greet_line, 0)
-    n_greet = n_sn - 1 + n_xl * n_xy - 1 + n_z * 2 - 1
+    n_greet = n_sn - 1 + n_xy + 2 * zh - jnp.where(z // zh == k, 2, 0) + jnp.where(t > 0, 1, 0)
 
     loads[0].wait()
     eye = lax.broadcasted_iota(jnp.int32, (cap, cap), 0) == lax.broadcasted_iota(jnp.int32, (cap, cap), 1)
@@ -122,17 +115,14 @@
         )
 
     def exchange(q):
-        def body(d, _):
+        for d in sorted(range(1, n_sn), key=lambda d: (-min(d // 2 % 4, 4 - d // 2 % 4), d)):
             a_copy(q, d).start()
-            return 0
-
-        lax.fori_loop(1, n_sn, body, 0)
         own = pl.ds(pl.multiple_of(s * cap, cap), cap)
         arr[q, own] = sendb[q, own]
 
     loads[2].wait()
     pick(0)
-    pl.semaphore_wait(barrier, n_greet + jnp.where(t > 0, 1, 0) + jnp.where(t < n_tm - 1, 1, 0))
+    pl.semaphore_wait(barrier, n_greet)
     exchange(0)
     exchange(1)
     loads[3].wait()
@@ -214,19 +204,56 @@
 
     place(0)
     place(1)
+    part(0, [0, 1], True)
+    part(1, [1], True)
     relay(0)
     place(2)
     relay(1)
     place(3)
+    part(0, [2, 3], False)
+    part(1, [2, 3], False)
+    relay(2)
+    part(2, [2, 3], True)
+    part(3, [3], True)
     for u in range(4):
-        part(u, list(range(u, 4)), True)
-    relay(2)
+        part(u, [4, 5], False)
     relay(3)
     for u in range(4):
-        part(u, [4, 5, 6, 7], False)
+        part(u, [6, 7], False)
 
     def out_copy(u):
         return pltpu.make_async_copy(hb.at[u], hank.at[pl.ds(8 * u, 8)], out_sem.at[u])
+
+    def s0_copy(a):
+        return pltpu.make_async_remote_copy(
+            src_ref=tot.at[a, pl.ds((1 - k) * zh, zh)],
+            dst_ref=s0b.at[a],
+            send_sem=s0_send.at[a],
+            recv_sem=s0_recv.at[a],
+            device_id=(t, s + 1 - 2 * k),
+            device_id_type=MESH,
+        )
+
+    def image(u, low, high):
+        lhs = jnp.concatenate(
+            [ht[LANES * u + 32 * v + low : LANES * u + 32 * v + high, :] for v in range(4)], axis=1
+        )
+        new = dot(lhs, rb[...])
+        acc2[low:high, :] = new if u == 0 else acc2[low:high, :] + new
+
+    half_span = span // n_xl
+
+    def grow(u):
+        if u < 3:
+            image(u, 0, span + INPUTS)
+            return
+        for a in range(n_xl):
+            low = half_span * a
+            image(u, low + INPUTS if a else 0, low + half_span + INPUTS)
+            whole = acc2[low : low + half_span, :LANES]
+            whole = whole + acc2[low + INPUTS : low + half_span + INPUTS, LANES:]
+            tot[a] = whole.reshape(tot.shape[1:])
+            s0_copy(a).start()
 
     for u in range(4):
         @pl.when(t < n_tm - 2)
@@ -244,27 +271,7 @@
             hb[u, 2 * v + 1] = r[:, LANES:]
             rb[v * sd : (v + 1) * sd, :] = r.astype(BF16)
         out_copy(u).start()
-        rows = span + INPUTS
-        lhs = jnp.concatenate([ht[LANES * u + 32 * v : LANES * u + 32 * v + rows, :] for v in range(4)], axis=1)
-        grown = dot(lhs, rb[...])
-        acc2[...] = grown if u == 0 else acc2[...] + grown
-
-    tr = tot.shape[3]
-    whole = acc2[:span, :LANES] + acc2[INPUTS : INPUTS + span, LANES:]
-    tot[...] = whole.reshape(tot.shape)
-
-    def s0_copy(a):
-        return pltpu.make_async_remote_copy(
-            src_ref=tot.at[a, pl.ds((1 - k) * zh, zh)],
-            dst_ref=s0b.at[a],
-            send_sem=s0_send.at[a],
-            recv_sem=s0_recv.at[a],
-            device_id=(t, s + 1 - 2 * k),
-            device_id_type=MESH,
-        )
-
-    for a in range(n_xl):
-        s0_copy(a).start()
+        grow(u)
 
     me = xl * n_xy + xy
 
@@ -293,16 +300,15 @@
         for c in range(zh):
             mid[a, :, c] = tot[a, k * zh + c] + s0b[a, c]
 
-        def body(d, _):
+        for d in sorted(range(n_xy), key=lambda d: -min(d % 4, 4 - d % 4)):
             b = lax.rem(xy + d, n_xy)
-
-            @pl.when((a != xl) | (b != xy))
-            def _():
+            if d:
                 s1_copy(a, b).start()
-
-            return 0
-
-        lax.fori_loop(0, n_xy, body, 0)
+            else:
+                @pl.when(a != xl)
+                def _():
+                    s1_copy(a, b).start()
+
 
     s1b[me] = mid[xl, xy]
 
@@ -349,7 +355,7 @@
             s2_arrival(e).wait_recv()
 
     done = jnp.sum(s2b[...], axis=0)
-    half = tr // 2
+    half = tot.shape[3] // 2
     col[...] = jnp.where(k == 0, done[:half], done[half:]) * scale
 
     for u in range(4):
@@ -387,6 +393,17 @@
             @pl.when((k * zh + c != z) | (k != kk))
             def _():
                 s2_copy(c, kk).wait_send()
+
+
+def flush(hank, col, hank_out, col_out, sems):
+    copies = [pltpu.make_async_copy(col, col_out, sems.at[0])]
+    for u in range(4):
+        part = pl.ds(8 * u, 8)
+        copies.append(pltpu.make_async_copy(hank.at[part], hank_out.at[part], sems.at[1 + u]))
+    for c in copies:
+        c.start()
+    for c in copies:
+        c.wait()
 
 
 def solution(mesh):
@@ -406,9 +423,9 @@
         tr = 2 * own_rows
         zh = n_z // 2
         scale = 1.0 / math.sqrt(sd * n_sn * steps * n_tm)
-        hbm = pl.BlockSpec(memory_space=pltpu.HBM)
+        hbm = pl.BlockSpec(memory_space=pl.ANY)
         dma = pltpu.SemaphoreType.DMA
-        return pl.pallas_call(
+        hank, col = pl.pallas_call(
             functools.partial(kernel, n_tm, n_sn, n_xl, 1, scale),
             out_shape=(
                 jax.ShapeDtypeStruct((steps, sd, cols), F32),
@@ -451,9 +468,20 @@
                 dma((n_z,)),
             ],
             compiler_params=pltpu.CompilerParams(
-                collective_id=0, has_side_effects=True, vmem_limit_bytes=63 * 2**20
+                collective_id=0, has_side_effects=True, vmem_limit_bytes=40 * 2**20
             ),
-        )(state, sketch, cell, row)
+        )(*[pltpu.with_memory_space_constraint(v, pltpu.HBM) for v in (state, sketch, cell, row)])
+        return pl.pallas_call(
+            flush,
+            out_shape=(
+                jax.ShapeDtypeStruct(hank.shape, F32),
+                jax.ShapeDtypeStruct(col.shape, F32),
+            ),
+            in_specs=[hbm] * 2,
+            out_specs=(hbm, hbm),
+            scratch_shapes=[dma((5,))],
+            compiler_params=pltpu.CompilerParams(vmem_limit_bytes=2**20),
+        )(hank, col)
 
     placed = (P("sensor", "tm"), P(), P("sensor", None, None), P("sensor", None, None))
     return jax.shard_map(

time: 54.8 us -> 52.3 us (0.954)
  local copies, waits for them, and re-layouts: 5.24 us -> 0 us
  Pallas kernels: 48.9 us -> 51.6 us
    unnamed x4 -> x0, local copies, waits for them, and re-layouts: 5.24 us -> none
    pallas_call x0 -> x1, Pallas kernels: none -> 2.05 us  [local(): pl.pallas_call(flush, out_shape=(jax.ShapeDtypeStruct(hank.shape, F32), j...]
    pallas_call x1, Pallas kernels: 48.9 us -> 49.5 us  [local(): pl.pallas_call(functools.partial(kernel, n_tm, n_sn, n_xl, 1, scale), out...]
where the time goes in v2:
time: 52.3 us; the launch traced here: 52.2 us
  Pallas kernels  51.6 us (99%)
  between operations  0.64 us (1%)
    pallas_call x1, Pallas kernels, local(): pl.pallas_call(functools.partial(kernel, n_tm, n_sn, n_xl, 1, scale), out...  49.5 us
    pallas_call x1, Pallas kernels, local(): pl.pallas_call(flush, out_shape=(jax.ShapeDtypeStruct(hank.shape, F32), j...  2.05 us

profile of v2, /device:TPU:1, one launch (start us, length us, event | category | flops | bytes accessed | tf_op | source)
XLA Modules:
  0.0 52.2 jit_solution(3866057433597854951)
XLA Ops:
  0.6 49.5 %shard_map.59 = (f32[32,256,128]{2,1,0:T(8,128)S(1)}, f32[4,128]{1,0:T(4,128)S(1)}) custom-call(bf16[2048,512]{1,0:T(8,128)(2,1)} %state.1, bf16[1024,128]{1,0:T(8,128)(2,1)} %sketch.1, s32[1,16,32]{2,1,0:T(8,128)} %cell.1, s32[1,16,32]{2,1,0:T(8,128)} %row.1), custom_call_target="tpu_custom_call" | custom-call | tf_op jit(solution)/shard_map/pallas_call | solution.py:428
  50.1 2.1 %shard_map.60 = (f32[32,256,128]{2,1,0:T(8,128)}, f32[4,128]{1,0:T(4,128)}) custom-call(f32[32,256,128]{2,1,0:T(8,128)S(1)} %get-tuple-element.4.hank, f32[4,128]{1,0:T(4,128)S(1)} %get-tuple-element.5.col), custom_call_target="tpu_custom_call" | custom-call | tf_op jit(solution)/shard_map/pallas_call | solution.py:474

commit v3 on v2

--- a/solution.py
+++ b/solution.py
@@ -206,14 +206,14 @@
     place(1)
     part(0, [0, 1], True)
     part(1, [1], True)
+    place(2)
+    place(3)
     relay(0)
-    place(2)
     relay(1)
-    place(3)
     part(0, [2, 3], False)
     part(1, [2, 3], False)
+    part(2, [2, 3], True)
     relay(2)
-    part(2, [2, 3], True)
     part(3, [3], True)
     for u in range(4):
         part(u, [4, 5], False)
@@ -261,9 +261,9 @@
             h_copy(4 + u).wait_recv()
             turn(8 + u)
 
-        chunks = list(range(8, 9 + u))
+        chunks = [8 + u] if u % 2 == 0 else [7 + u, 8 + u]
         lhs = jnp.concatenate([hx[c] for c in chunks], axis=1)
-        low = LANES * (8 - u)
+        low = LANES * (chunks[0] - u)
         for v in range(4):
             r = dot(lhs, big[low : low + LANES * len(chunks), 256 * v : 256 * v + 256])
             r = r + jnp.concatenate([hb[u, 2 * v], hb[u, 2 * v + 1]], axis=1)
@@ -272,6 +272,9 @@
             rb[v * sd : (v + 1) * sd, :] = r.astype(BF16)
         out_copy(u).start()
         grow(u)
+        if u == 1:
+            part(2, [8, 9], False)
+            part(3, [8, 9], False)
 
     me = xl * n_xy + xy
 
@@ -397,8 +400,8 @@
 
 def flush(hank, col, hank_out, col_out, sems):
     copies = [pltpu.make_async_copy(col, col_out, sems.at[0])]
-    for u in range(4):
-        part = pl.ds(8 * u, 8)
+    for u in range(16):
+        part = pl.ds(2 * u, 2)
         copies.append(pltpu.make_async_copy(hank.at[part], hank_out.at[part], sems.at[1 + u]))
     for c in copies:
         c.start()
@@ -479,7 +482,7 @@
             ),
             in_specs=[hbm] * 2,
             out_specs=(hbm, hbm),
-            scratch_shapes=[dma((5,))],
+            scratch_shapes=[dma((17,))],
             compiler_params=pltpu.CompilerParams(vmem_limit_bytes=2**20),
         )(hank, col)
 

time: 52.3 us -> 49.5 us (0.946)
  Pallas kernels: 51.6 us -> 48.8 us
    pallas_call x1, Pallas kernels: 49.5 us -> 46.6 us  [local(): pl.pallas_call(functools.partial(kernel, n_tm, n_sn, n_xl, 1, scale), out...]
where the time goes in v3:
time: 49.5 us; the launch traced here: 49.4 us
  Pallas kernels  48.8 us (99%)
  between operations  0.64 us (1%)
    pallas_call x1, Pallas kernels, local(): pl.pallas_call(functools.partial(kernel, n_tm, n_sn, n_xl, 1, scale), out...  46.6 us
    pallas_call x1, Pallas kernels, local(): pl.pallas_call(flush, out_shape=(jax.ShapeDtypeStruct(hank.shape, F32), j...  2.15 us

profile of v3, /device:TPU:1, one launch (start us, length us, event | category | flops | bytes accessed | tf_op | source)
XLA Modules:
  0.0 49.4 jit_solution(784370334696130079)
XLA Ops:
  0.6 46.6 %shard_map.59 = (f32[32,256,128]{2,1,0:T(8,128)S(1)}, f32[4,128]{1,0:T(4,128)S(1)}) custom-call(bf16[2048,512]{1,0:T(8,128)(2,1)} %state.1, bf16[1024,128]{1,0:T(8,128)(2,1)} %sketch.1, s32[1,16,32]{2,1,0:T(8,128)} %cell.1, s32[1,16,32]{2,1,0:T(8,128)} %row.1), custom_call_target="tpu_custom_call" | custom-call | tf_op jit(solution)/shard_map/pallas_call | solution.py:431
  47.3 2.1 %shard_map.60 = (f32[32,256,128]{2,1,0:T(8,128)}, f32[4,128]{1,0:T(4,128)}) custom-call(f32[32,256,128]{2,1,0:T(8,128)S(1)} %get-tuple-element.4.hank, f32[4,128]{1,0:T(4,128)S(1)} %get-tuple-element.5.col), custom_call_target="tpu_custom_call" | custom-call | tf_op jit(solution)/shard_map/pallas_call | solution.py:477

commit v4 on v3

--- a/solution.py
+++ b/solution.py
@@ -12,6 +12,8 @@
 KC = 64
 LANES = 128
 MESH = pl.DeviceIdType.MESH
+AHEAD = 3
+FIRST = 4 - AHEAD
 F32 = jnp.float32
 BF16 = jnp.bfloat16
 
@@ -75,7 +77,12 @@
     def _():
         greet(t + 1, s)
 
-    n_greet = n_sn - 1 + n_xy + 2 * zh - jnp.where(z // zh == k, 2, 0) + jnp.where(t > 0, 1, 0)
+    @pl.when(t > 0)
+    def _():
+        greet(t - 1, s)
+
+    n_greet = n_sn - 1 + n_xy + 2 * zh - jnp.where(z // zh == k, 2, 0)
+    n_greet = n_greet + jnp.where(t > 0, 1, 0) + jnp.where(t < n_tm - 1, 1, 0)
 
     loads[0].wait()
     eye = lax.broadcasted_iota(jnp.int32, (cap, cap), 0) == lax.broadcasted_iota(jnp.int32, (cap, cap), 1)
@@ -147,23 +154,36 @@
 
     @pl.when(t >= n_tm - 2)
     def _():
+        hx[12:16] = jnp.zeros((4, sd, LANES), BF16)
+        ht[12 * LANES :, :] = jnp.zeros((4 * LANES, sd), BF16)
+
+    @pl.when(t == n_tm - 1)
+    def _():
         hx[8:12] = jnp.zeros((4, sd, LANES), BF16)
-        ht[8 * LANES :, :] = jnp.zeros((4 * LANES, sd), BF16)
-
-    @pl.when(t == n_tm - 1)
-    def _():
-        hx[4:8] = jnp.zeros((4, sd, LANES), BF16)
-        ht[4 * LANES : 8 * LANES, :] = jnp.zeros((4 * LANES, sd), BF16)
-
-    def h_copy(c):
-        return pltpu.make_async_remote_copy(
-            src_ref=hx.at[c],
-            dst_ref=hx.at[c + 4],
-            send_sem=h_send.at[c],
-            recv_sem=h_recv.at[c],
-            device_id=(jnp.maximum(t - 1, 0), s),
-            device_id_type=MESH,
-        )
+        ht[8 * LANES : 12 * LANES, :] = jnp.zeros((4 * LANES, sd), BF16)
+
+    acc2[...] = jnp.zeros_like(acc2)
+
+    def h_copy(src, dst, sem, to):
+        return pltpu.make_async_remote_copy(
+            src_ref=hx.at[src],
+            dst_ref=hx.at[dst],
+            send_sem=h_send.at[sem],
+            recv_sem=h_recv.at[sem],
+            device_id=(to, s),
+            device_id_type=MESH,
+        )
+
+    before, after = jnp.maximum(t - 1, 0), jnp.minimum(t + 1, n_tm - 1)
+
+    def down(q):
+        return h_copy(4 + q, 8 + q, q, before)
+
+    def onward(q):
+        return h_copy(8 + q, 12 + q, 4 + q, before)
+
+    def up(q):
+        return h_copy(4 + q, q, 8 + q, after)
 
     def turn(c):
         ht[LANES * c : LANES * (c + 1), :] = jnp.transpose(hx[c])
@@ -174,55 +194,121 @@
             return 0
 
         lax.fori_loop(1, n_sn, body, 0)
-        hx[q] = dot(put[...], arr[q]).astype(BF16)
+        hx[4 + q] = dot(put[...], arr[q]).astype(BF16)
 
         @pl.when(t > 0)
         def _():
-            h_copy(q).start()
-
-        turn(q)
+            down(q).start()
+
+        if q >= FIRST:
+            @pl.when(t < n_tm - 1)
+            def _():
+                up(q).start()
+
+        turn(4 + q)
 
     def relay(q):
         @pl.when(t < n_tm - 1)
         def _():
-            h_copy(q).wait_recv()
+            down(q).wait_recv()
 
             @pl.when(t > 0)
             def _():
-                h_copy(4 + q).start()
-
-            turn(4 + q)
-
-    def part(u, chunks, first):
+                onward(q).start()
+
+            turn(8 + q)
+
+    def below(q):
+        up(q).wait_recv()
+        turn(q)
+
+    def above(q):
+        @pl.when(t < n_tm - 2)
+        def _():
+            onward(q).wait_recv()
+            if 12 + q < 16 - AHEAD:
+                turn(12 + q)
+
+    def weigh(g, chunks, v):
         lhs = jnp.concatenate([hx[c] for c in chunks], axis=1)
-        low = LANES * (chunks[0] - u)
+        low = LANES * (chunks[0] - g)
+        return dot(lhs, big[low : low + LANES * len(chunks), 256 * v : 256 * v + 256])
+
+    def part(g, chunks, first=False):
         for v in range(4):
-            r = dot(lhs, big[low : low + LANES * len(chunks), 256 * v : 256 * v + 256])
+            r = weigh(g, chunks, v)
             for i in range(2):
                 piece = r[:, LANES * i : LANES * (i + 1)]
-                hb[u, 2 * v + i] = piece if first else hb[u, 2 * v + i] + piece
+                hb[g, 2 * v + i] = piece if first else hb[g, 2 * v + i] + piece
+
+    def last_part(g, chunks, rounded, kept):
+        for v in range(4):
+            r = weigh(g, chunks, v) + jnp.concatenate([hb[g, 2 * v], hb[g, 2 * v + 1]], axis=1)
+            if kept:
+                hb[g, 2 * v] = r[:, :LANES]
+                hb[g, 2 * v + 1] = r[:, LANES:]
+            if rounded:
+                rb[v * sd : (v + 1) * sd, :] = r.astype(BF16)
+
+    def out_copy(u):
+        return pltpu.make_async_copy(hb.at[4 + u], hank.at[pl.ds(8 * u, 8)], out_sem.at[u])
+
+    def image(g, low, high):
+        lhs = jnp.concatenate(
+            [ht[LANES * g + 32 * v + low : LANES * g + 32 * v + high, :] for v in range(4)], axis=1
+        )
+        acc2[low:high, :] = acc2[low:high, :] + dot(lhs, rb[...])
+
+    full = span + INPUTS
+    shared = list(range(4, 8 - AHEAD))
+    ahead = list(range(FIRST, 4))
+    later = list(range(8 - AHEAD, 8))
 
     place(0)
     place(1)
-    part(0, [0, 1], True)
-    part(1, [1], True)
+    for g in ahead + shared[:2]:
+        part(g, [4, 5] if g < 5 else [5], True)
     place(2)
     place(3)
     relay(0)
+    for g in ahead:
+        part(g, [6, 7])
     relay(1)
-    part(0, [2, 3], False)
-    part(1, [2, 3], False)
-    part(2, [2, 3], True)
+    for g in shared:
+        part(g, [6, 7], g == 6)
+
+    @pl.when(t == n_tm - 1)
+    def _():
+        for g in later:
+            for v in range(4):
+                rb[v * sd : (v + 1) * sd, :] = weigh(g, list(range(g, 8)), v).astype(BF16)
+            image(g, 0, full)
+
+    for g in ahead + shared:
+        if g > 0:
+            part(g, [8, 9])
     relay(2)
-    part(3, [3], True)
-    for u in range(4):
-        part(u, [4, 5], False)
+
+    @pl.when(t > 0)
+    def _():
+        for q in range(FIRST, 4):
+            below(q)
+        for g in ahead[:-1]:
+            tail = [c for c in range(8, g + 9) if c > 9 or g == 0]
+            if tail:
+                part(g, tail)
+            last_part(g, list(range(g, 4)), True, False)
+            image(g, 0, full)
+
     relay(3)
-    for u in range(4):
-        part(u, [6, 7], False)
-
-    def out_copy(u):
-        return pltpu.make_async_copy(hb.at[u], hank.at[pl.ds(8 * u, 8)], out_sem.at[u])
+
+    @pl.when(t > 0)
+    def _():
+        part(3, [10, 11])
+        last_part(3, [3], True, False)
+        image(3, 0, full)
+
+    half_span = span // n_xl
 
     def s0_copy(a):
         return pltpu.make_async_remote_copy(
@@ -234,47 +320,24 @@
             device_id_type=MESH,
         )
 
-    def image(u, low, high):
-        lhs = jnp.concatenate(
-            [ht[LANES * u + 32 * v + low : LANES * u + 32 * v + high, :] for v in range(4)], axis=1
-        )
-        new = dot(lhs, rb[...])
-        acc2[low:high, :] = new if u == 0 else acc2[low:high, :] + new
-
-    half_span = span // n_xl
-
-    def grow(u):
-        if u < 3:
-            image(u, 0, span + INPUTS)
-            return
+    for g in shared:
+        part(g, [10, 11])
+        above(g - 4)
+        last_part(g, [12] if g == 4 else list(range(12, g + 9)), True, True)
+        out_copy(g - 4).start()
+        if g < shared[-1]:
+            image(g, 0, full)
+            continue
         for a in range(n_xl):
             low = half_span * a
-            image(u, low + INPUTS if a else 0, low + half_span + INPUTS)
+            image(g, low + INPUTS if a else 0, low + half_span + INPUTS)
             whole = acc2[low : low + half_span, :LANES]
             whole = whole + acc2[low + INPUTS : low + half_span + INPUTS, LANES:]
             tot[a] = whole.reshape(tot.shape[1:])
             s0_copy(a).start()
 
-    for u in range(4):
-        @pl.when(t < n_tm - 2)
-        def _():
-            h_copy(4 + u).wait_recv()
-            turn(8 + u)
-
-        chunks = [8 + u] if u % 2 == 0 else [7 + u, 8 + u]
-        lhs = jnp.concatenate([hx[c] for c in chunks], axis=1)
-        low = LANES * (chunks[0] - u)
-        for v in range(4):
-            r = dot(lhs, big[low : low + LANES * len(chunks), 256 * v : 256 * v + 256])
-            r = r + jnp.concatenate([hb[u, 2 * v], hb[u, 2 * v + 1]], axis=1)
-            hb[u, 2 * v] = r[:, :LANES]
-            hb[u, 2 * v + 1] = r[:, LANES:]
-            rb[v * sd : (v + 1) * sd, :] = r.astype(BF16)
-        out_copy(u).start()
-        grow(u)
-        if u == 1:
-            part(2, [8, 9], False)
-            part(3, [8, 9], False)
+    for g in later:
+        part(g, list(range(g, 8)), True)
 
     me = xl * n_xy + xy
 
@@ -314,6 +377,8 @@
 
 
     s1b[me] = mid[xl, xy]
+    for g in later:
+        part(g, [8, 9, 10, 11])
 
     def s1_wait(d, _):
         s1_arrival(lax.rem(me + d, n_xl * n_xy)).wait_recv()
@@ -351,6 +416,11 @@
     @pl.when(z // zh == k)
     def _():
         s2b[z] = m2[z - k * zh]
+
+    for g in later:
+        above(g - 4)
+        last_part(g, list(range(12, g + 9)), False, True)
+        out_copy(g - 4).start()
 
     for e in range(n_z):
         @pl.when((e != z) | (z // zh != k))
@@ -373,12 +443,17 @@
     @pl.when(t > 0)
     def _():
         for q in range(4):
-            h_copy(q).wait_send()
-
-    @pl.when((t > 0) & (t < n_tm - 1))
-    def _():
-        for q in range(4):
-            h_copy(4 + q).wait_send()
+            down(q).wait_send()
+
+    @pl.when(t < n_tm - 1)
+    def _():
+        for q in range(FIRST, 4):
+            up(q).wait_send()
+
+        @pl.when(t > 0)
+        def _():
+            for q in range(4):
+                onward(q).wait_send()
 
     for a in range(n_xl):
         s0_copy(a).wait_send()
@@ -445,10 +520,10 @@
                 pltpu.VMEM((sd, slots), BF16),
                 pltpu.VMEM((4, slots, LANES), BF16),
                 pltpu.VMEM((4, slots, LANES), BF16),
-                pltpu.VMEM((12, sd, LANES), BF16),
-                pltpu.VMEM((12 * LANES, sd), BF16),
+                pltpu.VMEM((16, sd, LANES), BF16),
+                pltpu.VMEM((16 * LANES, sd), BF16),
                 pltpu.VMEM((span + LANES, 8 * LANES), BF16),
-                pltpu.VMEM((4, 8, sd, LANES), F32),
+                pltpu.VMEM((8, 8, sd, LANES), F32),
                 pltpu.VMEM((4 * sd, 2 * LANES), BF16),
                 pltpu.VMEM((span + INPUTS, 2 * LANES), F32),
                 pltpu.VMEM((n_xl, n_z, n_xy, tr, LANES), F32),
@@ -460,8 +535,8 @@
                 dma((5,)),
                 dma((4, n_sn)),
                 dma((4, n_sn)),
-                dma((8,)),
-                dma((8,)),
+                dma((12,)),
+                dma((12,)),
                 dma((4,)),
                 dma((n_xl,)),
                 dma((n_xl,)),

time: 49.5 us -> 46.9 us (0.947)
  Pallas kernels: 48.8 us -> 46 us
    pallas_call x1, Pallas kernels: 46.6 us -> 43.9 us  [local(): pl.pallas_call(functools.partial(kernel, n_tm, n_sn, n_xl, 1, scale), out...]
where the time goes in v4:
time: 46.9 us; the launch traced here: 46.8 us
  Pallas kernels  46 us (98%)
  between operations  0.8 us (2%)
    pallas_call x1, Pallas kernels, local(): pl.pallas_call(functools.partial(kernel, n_tm, n_sn, n_xl, 1, scale), out...  43.9 us
    pallas_call x1, Pallas kernels, local(): pl.pallas_call(flush, out_shape=(jax.ShapeDtypeStruct(hank.shape, F32), j...  2.15 us

profile of v4, /device:TPU:1, one launch (start us, length us, event | category | flops | bytes accessed | tf_op | source)
XLA Modules:
  0.0 46.8 jit_solution(14239207487963729224)
XLA Ops:
  0.6 43.9 %shard_map.59 = (f32[32,256,128]{2,1,0:T(8,128)S(1)}, f32[4,128]{1,0:T(4,128)S(1)}) custom-call(bf16[2048,512]{1,0:T(8,128)(2,1)} %state.1, bf16[1024,128]{1,0:T(8,128)(2,1)} %sketch.1, s32[1,16,32]{2,1,0:T(8,128)} %cell.1, s32[1,16,32]{2,1,0:T(8,128)} %row.1), custom_call_target="tpu_custom_call" | custom-call | tf_op jit(solution)/shard_map/pallas_call | solution.py:506
  44.5 2.1 %shard_map.60 = (f32[32,256,128]{2,1,0:T(8,128)}, f32[4,128]{1,0:T(4,128)}) custom-call(f32[32,256,128]{2,1,0:T(8,128)S(1)} %get-tuple-element.4.hank, f32[4,128]{1,0:T(4,128)S(1)} %get-tuple-element.5.col), custom_call_target="tpu_custom_call" | custom-call | tf_op jit(solution)/shard_map/pallas_call | solution.py:552

commit v5 on v4

--- a/solution.py
+++ b/solution.py
@@ -231,8 +231,9 @@
 
     def weigh(g, chunks, v):
         lhs = jnp.concatenate([hx[c] for c in chunks], axis=1)
-        low = LANES * (chunks[0] - g)
-        return dot(lhs, big[low : low + LANES * len(chunks), 256 * v : 256 * v + 256])
+        cols = slice(256 * v, 256 * v + 256)
+        rhs = jnp.concatenate([big[LANES * (c - g) : LANES * (c - g + 1), cols] for c in chunks], axis=0)
+        return dot(lhs, rhs)
 
     def part(g, chunks, first=False):
         for v in range(4):
@@ -266,16 +267,22 @@
 
     place(0)
     place(1)
-    for g in ahead + shared[:2]:
-        part(g, [4, 5] if g < 5 else [5], True)
+    for g in ahead + shared:
+        part(g, [4, 5], True)
+    relay(0)
     place(2)
+    relay(1)
+    for g in ahead + shared:
+        part(g, [8, 9])
+
+    @pl.when(t > 0)
+    def _():
+        below(1)
+
     place(3)
-    relay(0)
-    for g in ahead:
+    for g in ahead + shared:
         part(g, [6, 7])
-    relay(1)
-    for g in shared:
-        part(g, [6, 7], g == 6)
+    relay(2)
 
     @pl.when(t == n_tm - 1)
     def _():
@@ -284,28 +291,26 @@
                 rb[v * sd : (v + 1) * sd, :] = weigh(g, list(range(g, 8)), v).astype(BF16)
             image(g, 0, full)
 
-    for g in ahead + shared:
-        if g > 0:
-            part(g, [8, 9])
-    relay(2)
+    above(0)
+    part(4, [10, 12])
 
     @pl.when(t > 0)
     def _():
-        for q in range(FIRST, 4):
-            below(q)
-        for g in ahead[:-1]:
-            tail = [c for c in range(8, g + 9) if c > 9 or g == 0]
-            if tail:
-                part(g, tail)
-            last_part(g, list(range(g, 4)), True, False)
-            image(g, 0, full)
+        below(2)
+        part(1, [1, 2])
+        part(2, [2, 10])
+        below(3)
+        last_part(1, [3], True, False)
+        image(1, 0, full)
 
     relay(3)
 
     @pl.when(t > 0)
     def _():
-        part(3, [10, 11])
-        last_part(3, [3], True, False)
+        last_part(2, [3], True, False)
+        image(2, 0, full)
+        part(3, [10])
+        last_part(3, [3, 11], True, False)
         image(3, 0, full)
 
     half_span = span // n_xl
@@ -321,9 +326,7 @@
         )
 
     for g in shared:
-        part(g, [10, 11])
-        above(g - 4)
-        last_part(g, [12] if g == 4 else list(range(12, g + 9)), True, True)
+        last_part(g, [11], True, True)
         out_copy(g - 4).start()
         if g < shared[-1]:
             image(g, 0, full)
@@ -336,8 +339,18 @@
             tot[a] = whole.reshape(tot.shape[1:])
             s0_copy(a).start()
 
-    for g in later:
-        part(g, list(range(g, 8)), True)
+    def part_later(rel, first):
+        lhs = jnp.concatenate(
+            [jnp.concatenate([hx[g + c] for c in rel], axis=1) for g in later], axis=0
+        )
+        for v in range(4):
+            r = dot(lhs, big[LANES * rel[0] : LANES * (rel[-1] + 1), 256 * v : 256 * v + 256])
+            for n, g in enumerate(later):
+                for i in range(2):
+                    piece = r[sd * n : sd * (n + 1), LANES * i : LANES * (i + 1)]
+                    hb[g, 2 * v + i] = piece if first else hb[g, 2 * v + i] + piece
+
+    part_later([0, 1], True)
 
     me = xl * n_xy + xy
 
@@ -377,8 +390,7 @@
 
 
     s1b[me] = mid[xl, xy]
-    for g in later:
-        part(g, [8, 9, 10, 11])
+    part_later([2, 3], False)
 
     def s1_wait(d, _):
         s1_arrival(lax.rem(me + d, n_xl * n_xy)).wait_recv()
@@ -419,7 +431,8 @@
 
     for g in later:
         above(g - 4)
-        last_part(g, list(range(12, g + 9)), False, True)
+    part_later([4, 5, 6, 7, 8], False)
+    for g in later:
         out_copy(g - 4).start()
 
     for e in range(n_z):

time: 46.9 us -> 49.7 us (1.060)
  Pallas kernels: 46 us -> 48.8 us
    pallas_call x1, Pallas kernels: 43.9 us -> 46.7 us  [local(): pl.pallas_call(functools.partial(kernel, n_tm, n_sn, n_xl, 1, scale), out...]
where the time goes in v5:
time: 49.7 us; the launch traced here: 49.6 us
  Pallas kernels  48.8 us (98%)
  between operations  0.8 us (2%)
    pallas_call x1, Pallas kernels, local(): pl.pallas_call(functools.partial(kernel, n_tm, n_sn, n_xl, 1, scale), out...  46.7 us
    pallas_call x1, Pallas kernels, local(): pl.pallas_call(flush, out_shape=(jax.ShapeDtypeStruct(hank.shape, F32), j...  2.15 us

profile of v5, /device:TPU:1, one launch (start us, length us, event | category | flops | bytes accessed | tf_op | source)
XLA Modules:
  0.0 49.6 jit_solution(10452289358839929742)
XLA Ops:
  0.6 46.7 %shard_map.59 = (f32[32,256,128]{2,1,0:T(8,128)S(1)}, f32[4,128]{1,0:T(4,128)S(1)}) custom-call(bf16[2048,512]{1,0:T(8,128)(2,1)} %state.1, bf16[1024,128]{1,0:T(8,128)(2,1)} %sketch.1, s32[1,16,32]{2,1,0:T(8,128)} %cell.1, s32[1,16,32]{2,1,0:T(8,128)} %row.1), custom_call_target="tpu_custom_call" | custom-call | tf_op jit(solution)/shard_map/pallas_call | solution.py:519
  47.3 2.1 %shard_map.60 = (f32[32,256,128]{2,1,0:T(8,128)}, f32[4,128]{1,0:T(4,128)}) custom-call(f32[32,256,128]{2,1,0:T(8,128)S(1)} %get-tuple-element.4.hank, f32[4,128]{1,0:T(4,128)S(1)} %get-tuple-element.5.col), custom_call_target="tpu_custom_call" | custom-call | tf_op jit(solution)/shard_map/pallas_call | solution.py:565

commit v6 on v5

--- a/solution.py
+++ b/solution.py
@@ -251,8 +251,10 @@
             if rounded:
                 rb[v * sd : (v + 1) * sd, :] = r.astype(BF16)
 
-    def out_copy(u):
-        return pltpu.make_async_copy(hb.at[4 + u], hank.at[pl.ds(8 * u, 8)], out_sem.at[u])
+    def out_copy(u, v):
+        return pltpu.make_async_copy(
+            hb.at[4 + u, pl.ds(2 * v, 2)], hank.at[pl.ds(8 * u + 2 * v, 2)], out_sem.at[u, v]
+        )
 
     def image(g, low, high):
         lhs = jnp.concatenate(
@@ -269,20 +271,14 @@
     place(1)
     for g in ahead + shared:
         part(g, [4, 5], True)
+    place(2)
+    place(3)
     relay(0)
-    place(2)
+    for g in ahead:
+        part(g, [6, 7])
     relay(1)
-    for g in ahead + shared:
-        part(g, [8, 9])
-
-    @pl.when(t > 0)
-    def _():
-        below(1)
-
-    place(3)
-    for g in ahead + shared:
+    for g in shared:
         part(g, [6, 7])
-    relay(2)
 
     @pl.when(t == n_tm - 1)
     def _():
@@ -291,11 +287,13 @@
                 rb[v * sd : (v + 1) * sd, :] = weigh(g, list(range(g, 8)), v).astype(BF16)
             image(g, 0, full)
 
-    above(0)
-    part(4, [10, 12])
+    for g in ahead + shared:
+        part(g, [8, 9])
+    relay(2)
 
     @pl.when(t > 0)
     def _():
+        below(1)
         below(2)
         part(1, [1, 2])
         part(2, [2, 10])
@@ -313,6 +311,9 @@
         last_part(3, [3, 11], True, False)
         image(3, 0, full)
 
+    part(4, [10, 11])
+    above(0)
+
     half_span = span // n_xl
 
     def s0_copy(a):
@@ -326,8 +327,9 @@
         )
 
     for g in shared:
-        last_part(g, [11], True, True)
-        out_copy(g - 4).start()
+        last_part(g, [12], True, True)
+        for v in range(4):
+            out_copy(g - 4, v).start()
         if g < shared[-1]:
             image(g, 0, full)
             continue
@@ -349,6 +351,8 @@
                 for i in range(2):
                     piece = r[sd * n : sd * (n + 1), LANES * i : LANES * (i + 1)]
                     hb[g, 2 * v + i] = piece if first else hb[g, 2 * v + i] + piece
+                if rel[-1] == 8:
+                    out_copy(g - 4, v).start()
 
     part_later([0, 1], True)
 
@@ -390,7 +394,7 @@
 
 
     s1b[me] = mid[xl, xy]
-    part_later([2, 3], False)
+    part_later([2, 3, 4, 5], False)
 
     def s1_wait(d, _):
         s1_arrival(lax.rem(me + d, n_xl * n_xy)).wait_recv()
@@ -431,9 +435,7 @@
 
     for g in later:
         above(g - 4)
-    part_later([4, 5, 6, 7, 8], False)
-    for g in later:
-        out_copy(g - 4).start()
+    part_later([6, 7, 8], False)
 
     for e in range(n_z):
         @pl.when((e != z) | (z // zh != k))
@@ -445,7 +447,8 @@
     col[...] = jnp.where(k == 0, done[:half], done[half:]) * scale
 
     for u in range(4):
-        out_copy(u).wait()
+        for v in range(4):
+            out_copy(u, v).wait()
     for q in range(4):
         def body(d, _):
             a_copy(q, d).wait_send()
@@ -550,7 +553,7 @@
                 dma((4, n_sn)),
                 dma((12,)),
                 dma((12,)),
-                dma((4,)),
+                dma((4, 4)),
                 dma((n_xl,)),
                 dma((n_xl,)),
                 dma((n_xl, n_xy)),

time: 49.7 us -> 46.8 us (0.942)
  Pallas kernels: 48.8 us -> 45.9 us
    pallas_call x1, Pallas kernels: 46.7 us -> 43.7 us  [local(): pl.pallas_call(functools.partial(kernel, n_tm, n_sn, n_xl, 1, scale), out...]
where the time goes in v6:
time: 46.8 us; the launch traced here: 46.7 us
  Pallas kernels  45.9 us (98%)
  between operations  0.8 us (2%)
    pallas_call x1, Pallas kernels, local(): pl.pallas_call(functools.partial(kernel, n_tm, n_sn, n_xl, 1, scale), out...  43.7 us
    pallas_call x1, Pallas kernels, local(): pl.pallas_call(flush, out_shape=(jax.ShapeDtypeStruct(hank.shape, F32), j...  2.15 us

profile of v6, /device:TPU:1, one launch (start us, length us, event | category | flops | bytes accessed | tf_op | source)
XLA Modules:
  0.0 46.7 jit_solution(14183496476534331096)
XLA Ops:
  0.6 43.7 %shard_map.59 = (f32[32,256,128]{2,1,0:T(8,128)S(1)}, f32[4,128]{1,0:T(4,128)S(1)}) custom-call(bf16[2048,512]{1,0:T(8,128)(2,1)} %state.1, bf16[1024,128]{1,0:T(8,128)(2,1)} %sketch.1, s32[1,16,32]{2,1,0:T(8,128)} %cell.1, s32[1,16,32]{2,1,0:T(8,128)} %row.1), custom_call_target="tpu_custom_call" | custom-call | tf_op jit(solution)/shard_map/pallas_call | solution.py:522
  44.4 2.1 %shard_map.60 = (f32[32,256,128]{2,1,0:T(8,128)}, f32[4,128]{1,0:T(4,128)}) custom-call(f32[32,256,128]{2,1,0:T(8,128)S(1)} %get-tuple-element.4.hank, f32[4,128]{1,0:T(4,128)S(1)} %get-tuple-element.5.col), custom_call_target="tpu_custom_call" | custom-call | tf_op jit(solution)/shard_map/pallas_call | solution.py:568

commit v7 on v6

--- a/solution.py
+++ b/solution.py
@@ -25,8 +25,8 @@
 def kernel(
     n_tm, n_sn, n_xl, n_xh, scale,
     state, sketch, cell, row, hank, col,
-    st, sk, cellv, rowv, one, put, sendb, arr, hx, ht, big, hb, rb, acc2, tot, s0b, mid, s1b, m2, s2b,
-    ld_sem, a_send, a_recv, h_send, h_recv, out_sem, s0_send, s0_recv, s1_send, s1_recv, s2_send, s2_recv,
+    st, sk, cellv, rowv, one, put, sendb, arr, hx, ht, big, hb, rb, acc2, tot, s0b, mid, s1b, m2, s2b, via,
+    ld_sem, a_send, a_recv, h_send, h_recv, out_sem, s0_send, s0_recv, s1_send, s1_recv, s2_send, s2_recv, via_send, via_recv,
 ):
     t = lax.axis_index("tm")
     s = lax.axis_index("sensor")
@@ -121,9 +121,45 @@
             device_id_type=MESH,
         )
 
+    detour = (4, 12) if n_sn == 16 else ()
+
+    def along(steps):
+        line = s // 8 * 4 + lax.rem(s // 2 + 4 + steps, 4)
+        return 2 * line + k
+
+    def via_copy(q, j):
+        dst = lax.rem(s + detour[j], n_sn)
+        return pltpu.make_async_remote_copy(
+            src_ref=sendb.at[q, pl.ds(pl.multiple_of(dst * cap, cap), cap)],
+            dst_ref=via.at[q, j],
+            send_sem=a_send.at[q, detour[j]],
+            recv_sem=via_recv.at[q, j],
+            device_id=(t, along(-1)),
+            device_id_type=MESH,
+        )
+
+    def pass_copy(q, j):
+        origin = along(1)
+        return pltpu.make_async_remote_copy(
+            src_ref=via.at[q, j],
+            dst_ref=arr.at[q, pl.ds(pl.multiple_of(origin * cap, cap), cap)],
+            send_sem=via_send.at[q, j],
+            recv_sem=a_recv.at[q, origin],
+            device_id=(t, lax.rem(origin + detour[j], n_sn)),
+            device_id_type=MESH,
+        )
+
+    def pass_on(q):
+        for j in range(len(detour)):
+            via_copy(q, j).wait_recv()
+            pass_copy(q, j).start()
+
     def exchange(q):
+        for j in range(len(detour)):
+            via_copy(q, j).start()
         for d in sorted(range(1, n_sn), key=lambda d: (-min(d // 2 % 4, 4 - d // 2 % 4), d)):
-            a_copy(q, d).start()
+            if d not in detour:
+                a_copy(q, d).start()
         own = pl.ds(pl.multiple_of(s * cap, cap), cap)
         arr[q, own] = sendb[q, own]
 
@@ -267,8 +303,12 @@
     ahead = list(range(FIRST, 4))
     later = list(range(8 - AHEAD, 8))
 
+    pass_on(0)
+    pass_on(1)
     place(0)
+    pass_on(2)
     place(1)
+    pass_on(3)
     for g in ahead + shared:
         part(g, [4, 5], True)
     place(2)
@@ -449,6 +489,9 @@
     for u in range(4):
         for v in range(4):
             out_copy(u, v).wait()
+    for q in range(4):
+        for j in range(len(detour)):
+            pass_copy(q, j).wait_send()
     for q in range(4):
         def body(d, _):
             a_copy(q, d).wait_send()
@@ -548,6 +591,7 @@
                 pltpu.VMEM((n_xl * n_xy, zh, tr, LANES), F32),
                 pltpu.VMEM((zh, tr, LANES), F32),
                 pltpu.VMEM((n_z, tr, LANES), F32),
+                pltpu.VMEM((4, 2, cap, LANES), BF16),
                 dma((5,)),
                 dma((4, n_sn)),
                 dma((4, n_sn)),
@@ -560,6 +604,8 @@
                 dma((n_xl * n_xy,)),
                 dma((zh, 2)),
                 dma((n_z,)),
+                dma((4, 2)),
+                dma((4, 2)),
             ],
             compiler_params=pltpu.CompilerParams(
                 collective_id=0, has_side_effects=True, vmem_limit_bytes=40 * 2**20

time: 46.8 us -> 52.9 us (1.13)
  Pallas kernels: 45.9 us -> 51.9 us
    pallas_call x1, Pallas kernels: 43.7 us -> 49.8 us  [local(): pl.pallas_call(functools.partial(kernel, n_tm, n_sn, n_xl, 1, scale), out...]
where the time goes in v7:
time: 52.9 us; the launch traced here: 52.7 us
  Pallas kernels  51.9 us (98%)
  between operations  0.8 us (2%)
    pallas_call x1, Pallas kernels, local(): pl.pallas_call(functools.partial(kernel, n_tm, n_sn, n_xl, 1, scale), out...  49.8 us
    pallas_call x1, Pallas kernels, local(): pl.pallas_call(flush, out_shape=(jax.ShapeDtypeStruct(hank.shape, F32), j...  2.15 us

profile of v7, /device:TPU:1, one launch (start us, length us, event | category | flops | bytes accessed | tf_op | source)
XLA Modules:
  0.0 52.7 jit_solution(14449588054510985339)
XLA Ops:
  0.6 49.8 %shard_map.59 = (f32[32,256,128]{2,1,0:T(8,128)S(1)}, f32[4,128]{1,0:T(4,128)S(1)}) custom-call(bf16[2048,512]{1,0:T(8,128)(2,1)} %state.1, bf16[1024,128]{1,0:T(8,128)(2,1)} %sketch.1, s32[1,16,32]{2,1,0:T(8,128)} %cell.1, s32[1,16,32]{2,1,0:T(8,128)} %row.1), custom_call_target="tpu_custom_call" | custom-call | tf_op jit(solution)/shard_map/pallas_call | solution.py:565
  50.4 2.1 %shard_map.60 = (f32[32,256,128]{2,1,0:T(8,128)}, f32[4,128]{1,0:T(4,128)}) custom-call(f32[32,256,128]{2,1,0:T(8,128)S(1)} %get-tuple-element.4.hank, f32[4,128]{1,0:T(4,128)S(1)} %get-tuple-element.5.col), custom_call_target="tpu_custom_call" | custom-call | tf_op jit(solution)/shard_map/pallas_call | solution.py:614

commit v8 on v6

--- a/solution.py
+++ b/solution.py
@@ -437,6 +437,40 @@
         above(g - 4)
     part_later([6, 7, 8], False)
 
+    for q in range(4):
+        def body(d, _):
+            a_copy(q, d).wait_send()
+            return 0
+
+        lax.fori_loop(1, n_sn, body, 0)
+
+    @pl.when(t > 0)
+    def _():
+        for q in range(4):
+            down(q).wait_send()
+
+    @pl.when(t < n_tm - 1)
+    def _():
+        for q in range(FIRST, 4):
+            up(q).wait_send()
+
+        @pl.when(t > 0)
+        def _():
+            for q in range(4):
+                onward(q).wait_send()
+
+    for a in range(n_xl):
+        s0_copy(a).wait_send()
+
+        def body(b, _):
+            @pl.when((a != xl) | (b != xy))
+            def _():
+                s1_copy(a, b).wait_send()
+
+            return 0
+
+        lax.fori_loop(0, n_xy, body, 0)
+
     for e in range(n_z):
         @pl.when((e != z) | (z // zh != k))
         def _():
@@ -449,39 +483,6 @@
     for u in range(4):
         for v in range(4):
             out_copy(u, v).wait()
-    for q in range(4):
-        def body(d, _):
-            a_copy(q, d).wait_send()
-            return 0
-
-        lax.fori_loop(1, n_sn, body, 0)
-
-    @pl.when(t > 0)
-    def _():
-        for q in range(4):
-            down(q).wait_send()
-
-    @pl.when(t < n_tm - 1)
-    def _():
-        for q in range(FIRST, 4):
-            up(q).wait_send()
-
-        @pl.when(t > 0)
-        def _():
-            for q in range(4):
-                onward(q).wait_send()
-
-    for a in range(n_xl):
-        s0_copy(a).wait_send()
-
-        def body(b, _):
-            @pl.when((a != xl) | (b != xy))
-            def _():
-                s1_copy(a, b).wait_send()
-
-            return 0
-
-        lax.fori_loop(0, n_xy, body, 0)
     for c in range(zh):
         for kk in range(2):
             @pl.when((k * zh + c != z) | (k != kk))

time: 46.8 us -> 46.2 us (0.987)
  Pallas kernels: 45.9 us -> 45.3 us
    pallas_call x1, Pallas kernels: 43.7 us -> 43.2 us  [local(): pl.pallas_call(functools.partial(kernel, n_tm, n_sn, n_xl, 1, scale), out...]
where the time goes in v8:
time: 46.2 us; the launch traced here: 46.1 us
  Pallas kernels  45.3 us (98%)
  between operations  0.8 us (2%)
    pallas_call x1, Pallas kernels, local(): pl.pallas_call(functools.partial(kernel, n_tm, n_sn, n_xl, 1, scale), out...  43.2 us
    pallas_call x1, Pallas kernels, local(): pl.pallas_call(flush, out_shape=(jax.ShapeDtypeStruct(hank.shape, F32), j...  2.15 us

profile of v8, /device:TPU:1, one launch (start us, length us, event | category | flops | bytes accessed | tf_op | source)
XLA Modules:
  0.0 46.1 jit_solution(10601664623730886755)
XLA Ops:
  0.6 43.2 %shard_map.59 = (f32[32,256,128]{2,1,0:T(8,128)S(1)}, f32[4,128]{1,0:T(4,128)S(1)}) custom-call(bf16[2048,512]{1,0:T(8,128)(2,1)} %state.1, bf16[1024,128]{1,0:T(8,128)(2,1)} %sketch.1, s32[1,16,32]{2,1,0:T(8,128)} %cell.1, s32[1,16,32]{2,1,0:T(8,128)} %row.1), custom_call_target="tpu_custom_call" | custom-call | tf_op jit(solution)/shard_map/pallas_call | solution.py:523
  43.8 2.1 %shard_map.60 = (f32[32,256,128]{2,1,0:T(8,128)}, f32[4,128]{1,0:T(4,128)}) custom-call(f32[32,256,128]{2,1,0:T(8,128)S(1)} %get-tuple-element.4.hank, f32[4,128]{1,0:T(4,128)S(1)} %get-tuple-element.5.col), custom_call_target="tpu_custom_call" | custom-call | tf_op jit(solution)/shard_map/pallas_call | solution.py:569
